TPU v7x, 512 devices: a whole 4x8x8 slice. The times are simulated.
512 devices in a mesh: dp: 16 (over z, core), expert: 32 (over x, y).
Axes of the slice: x: 4, y: 8, z: 8, core: 2. Of those that a mesh axis runs over, the one named last changes fastest.
Arguments:
- layer_input: bfloat16 [1280, 4096], P('expert', 'dp'), may hold values from -6 to 6
- output_grad: bfloat16 [1280, 4096], P('expert', 'dp'), may hold values from -3 to 3
- route_ids: int32 [1280, 8], P('expert'), may hold values from 0 to 31, all different within a row; in each aligned block of 40 rows (0 to 39, 40 to 79, ...) at most 15 rows name the same one
- route_probs: bfloat16 [1280, 8], P('expert'), may hold values from 0.049804688 to 0.3984375
- gate_weight: bfloat16 [32, 4096, 1024], P('expert', 'dp'), may hold values from -0.09375 to 0.09375
- up_weight: bfloat16 [32, 4096, 1024], P('expert', 'dp'), may hold values from -0.09375 to 0.09375
- down_weight: bfloat16 [32, 1024, 4096], P('expert', None, 'dp'), may hold values from -0.1875 to 0.1875
Outputs:
- input_grad: bfloat16 [1280, 4096], P('expert', 'dp')
- prob_grad: bfloat16 [1280, 8], P('expert')
- gate_grad: bfloat16 [32, 4096, 1024], P('expert', 'dp')
- up_grad: bfloat16 [32, 4096, 1024], P('expert', 'dp')
- down_grad: bfloat16 [32, 1024, 4096], P('expert', None, 'dp')
Inputs may be any that keep to these rules, and one draw needn't show every extreme that they name: `route_ids`: each token names 8 different experts. In each aligned block of 40 tokens (the tokens of one index of the expert axis) at most 15 tokens name the same expert, and in every draw some expert is named by exactly 15 tokens of some block.
All inputs are finite; a program needn't handle non-finite values.
Results may differ from a plain program's by a relative error of at most 0.035.
Values may be sent and summed in bfloat16 or wider, within the bound.
A program may use at most 64 MiB of HBM per device.

v0:
```python
import jax
import jax.numpy as jnp
from jax import lax
from jax.sharding import PartitionSpec as P


def swiglu_back(gate_pre, up_pre, hidden_grad):
    sig_gate = jax.nn.sigmoid(gate_pre)
    active = (gate_pre * sig_gate * up_pre).astype(jnp.bfloat16)
    gate_delta = (hidden_grad * up_pre * sig_gate * (1.0 + gate_pre * (1.0 - sig_gate))).astype(
        jnp.bfloat16
    )
    up_delta = (hidden_grad * gate_pre * sig_gate).astype(jnp.bfloat16)
    return (active, gate_delta, up_delta)


def contract_last(left, right):
    return lax.dot_general(
        left, right, (((1,), (1,)), ((), ())), preferred_element_type=jnp.float32
    )


def on_device(
    layer_input, output_grad, route_ids, route_probs, gate_weight, up_weight, down_weight
):
    tok_count = layer_input.shape[0]
    width_part = layer_input.shape[1]
    chosen = route_ids.shape[1]
    experts = lax.axis_size("expert")
    capacity = 3 * tok_count * chosen // (2 * experts)
    row_count = experts * capacity
    cslots = jnp.arange(capacity, dtype=jnp.int32)
    expert_ids = jnp.arange(experts, dtype=jnp.int32)
    onehot = (route_ids[:, :, None] == expert_ids).astype(jnp.int32)
    member = jnp.sum(onehot, axis=1)
    before = jnp.cumsum(member, axis=0) - member
    pweight = jnp.sum(
        onehot.astype(jnp.float32) * route_probs.astype(jnp.float32)[:, :, None], axis=1
    )
    select = ((before[:, :, None] == cslots) & (member[:, :, None] > 0)).astype(jnp.bfloat16)
    send_x = jnp.einsum(
        "tec,td->ecd", select, layer_input, preferred_element_type=jnp.float32
    ).astype(jnp.bfloat16)
    send_g = jnp.einsum(
        "tec,td->ecd", select, output_grad, preferred_element_type=jnp.float32
    ).astype(jnp.bfloat16)
    send_p = jnp.einsum("tec,te->ec", select.astype(jnp.float32), pweight).astype(jnp.bfloat16)
    recv_x, recv_g, recv_p = (
        lax.all_to_all(send_x, "expert", split_axis=0, concat_axis=0, tiled=True),
        lax.all_to_all(send_g, "expert", split_axis=0, concat_axis=0, tiled=True),
        lax.all_to_all(send_p, "expert", split_axis=0, concat_axis=0, tiled=True),
    )
    rows_x = recv_x.reshape(row_count, width_part)
    rows_g = recv_g.reshape(row_count, width_part)
    rows_p = recv_p.reshape(row_count)
    gate_w = gate_weight[0]
    up_w = up_weight[0]
    down_w = down_weight[0]
    scaled = (rows_p.astype(jnp.float32)[:, None] * rows_g.astype(jnp.float32)).astype(jnp.bfloat16)
    gate_part = jnp.dot(rows_x, gate_w, preferred_element_type=jnp.float32)
    up_part = jnp.dot(rows_x, up_w, preferred_element_type=jnp.float32)
    grad_part = contract_last(scaled, down_w)
    gate_pre, up_pre, hidden_grad = (
        lax.psum(gate_part.astype(jnp.bfloat16), "dp").astype(jnp.float32),
        lax.psum(up_part.astype(jnp.bfloat16), "dp").astype(jnp.float32),
        lax.psum(grad_part.astype(jnp.bfloat16), "dp").astype(jnp.float32),
    )
    active, gate_delta, up_delta = swiglu_back(gate_pre, up_pre, hidden_grad)
    out_rows = jnp.dot(active, down_w, preferred_element_type=jnp.float32)
    dot_part = jnp.sum(rows_g.astype(jnp.float32) * out_rows, axis=1)
    gate_dot = lax.psum(dot_part, "dp").astype(jnp.bfloat16)
    down_grad = jnp.einsum("rf,rd->fd", active, scaled, preferred_element_type=jnp.float32).astype(
        jnp.bfloat16
    )[None]
    gate_grad = jnp.einsum(
        "rd,rf->df", rows_x, gate_delta, preferred_element_type=jnp.float32
    ).astype(jnp.bfloat16)[None]
    up_grad = jnp.einsum("rd,rf->df", rows_x, up_delta, preferred_element_type=jnp.float32).astype(
        jnp.bfloat16
    )[None]
    row_grad = (contract_last(gate_delta, gate_w) + contract_last(up_delta, up_w)).astype(
        jnp.bfloat16
    )
    back_x, back_p = (
        lax.all_to_all(
            row_grad.reshape(experts, capacity, width_part),
            "expert",
            split_axis=0,
            concat_axis=0,
            tiled=True,
        ),
        lax.all_to_all(
            gate_dot.reshape(experts, capacity), "expert", split_axis=0, concat_axis=0, tiled=True
        ),
    )
    input_sum = jnp.einsum("tec,ecd->td", select, back_x, preferred_element_type=jnp.float32)
    gate_table = jnp.einsum("tec,ec->te", select.astype(jnp.float32), back_p.astype(jnp.float32))
    input_grad = input_sum.astype(jnp.bfloat16)
    prob_grad = jnp.sum(onehot.astype(jnp.float32) * gate_table[:, None, :], axis=2).astype(
        jnp.bfloat16
    )
    return (input_grad, prob_grad, gate_grad, up_grad, down_grad)


def solution(mesh):
    placed = (
        P("expert", "dp"),
        P("expert", "dp"),
        P("expert", None),
        P("expert", None),
        P("expert", "dp", None),
        P("expert", "dp", None),
        P("expert", None, "dp"),
    )
    return jax.shard_map(
        on_device,
        mesh=mesh,
        in_specs=placed,
        out_specs=(
            P("expert", "dp"),
            P("expert", None),
            P("expert", "dp", None),
            P("expert", "dp", None),
            P("expert", None, "dp"),
        ),
        check_vma=False,
    )
```

profile of v0, /device:TPU:8, one launch (start us, length us, event | category | flops | bytes accessed | tf_op | source)
XLA Modules:
  0.0 364.9 jit_solution(10696455717776967576)
XLA Ops:
  7.2 0.0 copy-start
  7.2 0.0 all-reduce.6.cloned.1.call-start
  7.2 0.8 convert_reduce_fusion
  8.0 0.1 copy.46
  8.1 0.1 reduce_window_sum.11
  8.2 0.1 copy.48
  8.2 0.9 convolution_convert_fusion.6
  9.2 0.1 copy.51
  9.3 22.2 %all_to_all.37 = bf16[32,15,256]{2,1,0:T(8,128)(2,1)S(1)} all-to-all(bf16[32,15,256]{2,1,0:T(8,128)(2,1)S(1)} %copy.51), channel_id=1, replica_groups=mesh['dp'=16,'expert'=32] {'expert'}, dimensions={0} | all-to-all | bytes 491520 | tf_op jit(solution)/shard_map/all_to_all | solution.py:49
  31.6 0.1 reshape.59
  31.6 0.0 copy-done
  31.7 0.0 copy-start.3
  31.7 1.4 convolution_convert_fusion
  33.0 0.0 copy-done.3
  33.0 1.4 convolution_convert_fusion.1
  34.4 0.0 copy-start.6
  34.4 0.0 all-reduce.6.cloned.1.call-update
  34.4 0.7 copy-done.6
  35.1 0.2 convolution_convert_fusion.7
  35.4 0.1 copy.50
  35.5 15.8 %all_to_all.38 = bf16[32,15,256]{2,1,0:T(8,128)(2,1)S(1)} all-to-all(bf16[32,15,256]{2,1,0:T(8,128)(2,1)S(1)} %copy.50), channel_id=1, replica_groups=mesh['dp'=16,'expert'=32] {'expert'}, dimensions={0} | all-to-all | bytes 491520 | tf_op jit(solution)/shard_map/all_to_all | solution.py:50
  51.4 0.1 reshape.62
  51.4 0.0 copy-start.4
  51.4 103.7 %all-reduce.6.cloned.1.call-done = (bf16[480,1024]{1,0:T(8,128)(2,1)}, bf16[480,1024]{1,0:T(8,128)(2,1)}) async-done(((bf16[480,1024]{1,0:T(8,128)(2,1)}, bf16[480,1024]{1,0:T(8,128)(2,1)}), (bf16[480,1024]{1,0:T(8,128)(2,1)}, bf16[480,1024]{1,0:T(8,128)(2,1)})) %all-reduce.6.cloned.1.call-update) | async-done | bytes 1966096 | tf_op jit(solution)/shard_map/psum | solution.py:65
  155.2 2.2 fusion.3
  157.4 0.0 copy-done.4
  157.4 0.0 copy-start.1
  157.4 0.9 copy-done.1
  158.3 0.0 copy-done.2
  158.3 0.5 fusion.14
  158.8 26.2 %psum.31 = bf16[480]{0:T(512)(128)(2,1)S(1)} all-reduce(f32[480]{0:T(512)S(1)} %fusion.14), channel_id=1, replica_groups=mesh['dp'=16,'expert'=32] {'dp'}, use_global_device_ids=true, to_apply=%region_7.8 | all-reduce | flops 480 | bytes 2880 | tf_op jit(solution)/shard_map/psum | solution.py:71
  185.1 0.7 all_to_all.31
  185.8 9.9 %all-to-all-start.4 = ((bf16[32,1,15]{2,1,0:T(2,128)(2,1)}), bf16[32,1,15]{2,1,0:T(2,128)(2,1)S(1)}, u32[]{:S(2)}, u32[]{:S(2)}) async-start(bf16[32,1,15]{2,1,0:T(2,128)(2,1)} %all_to_all.31), calls=%async_computation.4 | async-start | bytes 32768 | tf_op jit(solution)/shard_map/all_to_all | solution.py:92
  195.7 0.0 all-reduce.4.cloned.1.call-start
  195.8 0.0 copy-done.8
  195.8 8.4 %all-to-all-done.4 = bf16[32,1,15]{2,1,0:T(2,128)(2,1)S(1)} async-done(((bf16[32,1,15]{2,1,0:T(2,128)(2,1)}), bf16[32,1,15]{2,1,0:T(2,128)(2,1)S(1)}, u32[]{:S(2)}, u32[]{:S(2)}) %all-to-all-start.4) | async-done | bytes 992 | tf_op jit(solution)/shard_map/all_to_all | solution.py:92
  204.2 0.1 copy.54
  204.3 0.1 copy.58
  204.4 0.2 fusion.26
  204.6 0.0 copy-done.7
  204.6 0.6 fusion.33
  205.3 0.2 fusion.28
  205.5 0.1 copy.57
  205.6 0.1 copy.49
  205.7 12.8 %all_to_all.39 = bf16[32,1,15]{2,1,0:T(2,128)(2,1)S(1)} all-to-all(bf16[32,1,15]{2,1,0:T(2,128)(2,1)S(1)} %copy.49), channel_id=1, replica_groups=mesh['dp'=16,'expert'=32] {'expert'}, dimensions={0} | all-to-all | bytes 1920 | tf_op jit(solution)/shard_map/all_to_all | solution.py:51
  218.5 0.1 multiply_convert_fusion
  218.6 0.1 convert_element_type.114
  218.7 1.4 convolution_convert_fusion.2
  220.1 0.0 all-reduce.4.cloned.1.call-update
  220.2 0.1 convert_reduce_fusion.1
  220.2 0.1 reshape.63
  220.3 110.3 %all-reduce.4.cloned.1.call-done = bf16[480,1024]{1,0:T(8,128)(2,1)} async-done(((bf16[480,1024]{1,0:T(8,128)(2,1)}), bf16[480,1024]{1,0:T(8,128)(2,1)}) %all-reduce.4.cloned.1.call-update) | async-done | bytes 983056 | tf_op jit(solution)/shard_map/psum | solution.py:66
  330.6 2.8 fusion.9
  333.5 0.5 fusion.16
  333.9 0.5 fusion.13
  334.4 0.0 copy-start.5
  334.4 0.8 reshape.60
  335.2 9.9 %all-to-all-start.3 = ((bf16[32,15,256]{2,1,0:T(8,128)(2,1)}), bf16[32,15,256]{2,1,0:T(8,128)(2,1)}, u32[]{:S(2)}, u32[]{:S(2)}) async-start(bf16[32,15,256]{2,1,0:T(8,128)(2,1)} %reshape.60), calls=%async_computation.3 | async-start | bytes 524288 | tf_op jit(solution)/shard_map/all_to_all | solution.py:85
  345.1 0.0 copy-done.5
  345.1 2.6 fusion.12
  347.7 1.3 fusion.10
  348.9 1.3 fusion.11
  350.2 6.1 %all-to-all-done.3 = bf16[32,15,256]{2,1,0:T(8,128)(2,1)} async-done(((bf16[32,15,256]{2,1,0:T(8,128)(2,1)}), bf16[32,15,256]{2,1,0:T(8,128)(2,1)}, u32[]{:S(2)}, u32[]{:S(2)}) %all-to-all-start.3) | async-done | bytes 245792 | tf_op jit(solution)/shard_map/all_to_all | solution.py:85
  356.3 1.8 fusion.15
  (9 shorter events, 0.1 us)
Async XLA Ops:
  7.2 24.5 %copy-start = (bf16[1,256,1024]{2,1,0:T(8,128)(2,1)S(1)}, bf16[1,256,1024]{2,1,0:T(8,128)(2,1)}, u32[]{:S(2)}) copy-start(bf16[1,256,1024]{2,1,0:T(8,128)(2,1)} %param.11) | copy-start | bytes 1572868
  7.2 148.0 %all-reduce.6.cloned.1.call-start = ((), (), s32[]{:S(2)}) async-start(), calls=%async_computation.6 | async-start | bytes 3932160 | tf_op jit(solution)/shard_map/psum | solution.py:65
  31.7 1.4 copy-start.3
  34.4 0.7 copy-start.6
  51.4 105.9 %copy-start.4 = (f32[480,256]{1,0:T(8,128)}, f32[480,256]{1,0:T(8,128)S(1)}, u32[]{:S(2)}) copy-start(f32[480,256]{1,0:T(8,128)S(1)} %reshape.62) | copy-start | bytes 1474564
  155.2 3.2 copy-start.2
  157.4 1.0 copy-start.1
  158.3 37.4 %copy-start.8 = (bf16[40,8]{0,1:T(8,128)(2,1)S(1)}, bf16[40,8]{0,1:T(8,128)(2,1)}, u32[]{:S(2)}) copy-start(bf16[40,8]{0,1:T(8,128)(2,1)} %param.10) | copy-start | bytes 1924
  158.3 46.3 %copy-start.7 = (s32[40,8]{0,1:T(8,128)S(1)}, s32[40,8]{0,1:T(8,128)}, u32[]{:S(2)}) copy-start(s32[40,8]{0,1:T(8,128)} %param.9) | copy-start | bytes 3844
  185.8 18.4 %all-to-all-start.4 = ((bf16[32,1,15]{2,1,0:T(2,128)(2,1)}), bf16[32,1,15]{2,1,0:T(2,128)(2,1)S(1)}, u32[]{:S(2)}, u32[]{:S(2)}) async-start(bf16[32,1,15]{2,1,0:T(2,128)(2,1)} %all_to_all.31), calls=%async_computation.4 | async-start | bytes 32768 | tf_op jit(solution)/shard_map/all_to_all | solution.py:92
  195.7 135.0 %all-reduce.4.cloned.1.call-start = ((), (), s32[]{:S(2)}) async-start(), calls=%async_computation.5 | async-start | bytes 1966080 | tf_op jit(solution)/shard_map/psum | solution.py:66
  334.4 10.7 %copy-start.5 = (f32[480,256]{1,0:T(8,128)S(1)}, f32[480,256]{1,0:T(8,128)}, u32[]{:S(2)}) copy-start(f32[480,256]{1,0:T(8,128)} %copy-done.4) | copy-start | bytes 1474564
  335.2 21.1 %all-to-all-start.3 = ((bf16[32,15,256]{2,1,0:T(8,128)(2,1)}), bf16[32,15,256]{2,1,0:T(8,128)(2,1)}, u32[]{:S(2)}, u32[]{:S(2)}) async-start(bf16[32,15,256]{2,1,0:T(8,128)(2,1)} %reshape.60), calls=%async_computation.3 | async-start | bytes 524288 | tf_op jit(solution)/shard_map/all_to_all | solution.py:85
Sparse Core Ops, SparseCore 0:
  34.6 120.5 all-reduce.5
  220.3 110.3 all-reduce.3
where the time goes:
time: 366 us; the launch traced here: 365 us
  waiting for transfers between devices  229 us (63%)
  blocking collectives  77.1 us (21%)
  starting transfers between devices  19.8 us (5%)
  between operations  14.3 us (4%)
  matrix products  14 us (4%)
  other arithmetic  6.74 us (2%)
  local copies, waits for them, and re-layouts  4.39 us (1%)
    psum x1, waiting for transfers between devices, on_device(): lax.psum(grad_part.astype(jnp.bfloat16), 'dp').astype(jnp.float32)  110 us
    psum x1, waiting for transfers between devices, on_device(): lax.psum(up_part.astype(jnp.bfloat16), 'dp').astype(jnp.float32)  104 us
    psum x1, blocking collectives, on_device(): gate_dot = lax.psum(dot_part, 'dp').astype(jnp.bfloat16)  26.2 us
    all_to_all x1, blocking collectives, on_device(): lax.all_to_all(send_x, 'expert', split_axis=0, concat_axis=0, tiled=True)  22.2 us
    all_to_all x1, blocking collectives, on_device(): lax.all_to_all(send_g, 'expert', split_axis=0, concat_axis=0, tiled=True)  15.8 us
    all_to_all x1, blocking collectives, on_device(): lax.all_to_all(send_p, 'expert', split_axis=0, concat_axis=0, tiled=True)  12.8 us
    all_to_all x1, starting transfers between devices, on_device(): lax.all_to_all(row_grad.reshape(experts, capacity, width_part), 'expert',...  9.9 us
    all_to_all x1, starting transfers between devices, on_device(): lax.all_to_all(gate_dot.reshape(experts, capacity), 'expert', split_axis=...  9.85 us
  transfers between devices with their start and end apart: 4, of which 4 were waited for; matrix products, arithmetic and copies ran while one was open for 2% of the time, Pallas kernels for 0%

commit v1 on v0

--- a/solution.py
+++ b/solution.py
@@ -63,7 +63,7 @@
     gate_pre, up_pre, hidden_grad = (
         lax.psum(gate_part.astype(jnp.bfloat16), "dp").astype(jnp.float32),
         lax.psum(up_part.astype(jnp.bfloat16), "dp").astype(jnp.float32),
-        lax.psum(grad_part.astype(jnp.bfloat16), "dp").astype(jnp.float32),
+        jnp.sum(lax.all_gather(grad_part.astype(jnp.bfloat16), "dp"), axis=0).astype(jnp.float32),
     )
     active, gate_delta, up_delta = swiglu_back(gate_pre, up_pre, hidden_grad)
     out_rows = jnp.dot(active, down_w, preferred_element_type=jnp.float32)

time: 366 us -> 351 us (0.959)
  waiting for transfers between devices: 229 us -> 206 us
  other arithmetic: 6.74 us -> 16.5 us
    psum x1 -> x0, waiting for transfers between devices: 110 us -> none  [on_device(): lax.psum(grad_part.astype(jnp.bfloat16), 'dp').astype(jnp.float32)]
    all_gather x0 -> x1, waiting for transfers between devices: none -> 86.1 us  [on_device(): lax.all_gather(grad_part.astype(jnp.bfloat16), 'dp')]
    reduce_sum x0 -> x1, other arithmetic: none -> 9.72 us  [on_device(): jnp.sum(lax.all_gather(grad_part.astype(jnp.bfloat16), 'dp'), axis=0)]
where the time goes in v1:
time: 351 us
  waiting for transfers between devices  206 us (59%)
  blocking collectives  77.1 us (22%)
  starting transfers between devices  19.8 us (6%)
  other arithmetic  16.5 us (5%)
  between operations  14.3 us (4%)
  matrix products  13.2 us (4%)
  local copies, waits for them, and re-layouts  3.68 us (1%)
    psum x1, waiting for transfers between devices, on_device(): lax.psum(up_part.astype(jnp.bfloat16), 'dp').astype(jnp.float32)  104 us
    all_gather x1, waiting for transfers between devices, on_device(): lax.all_gather(grad_part.astype(jnp.bfloat16), 'dp')  86.1 us
    psum x1, blocking collectives, on_device(): gate_dot = lax.psum(dot_part, 'dp').astype(jnp.bfloat16)  26.2 us
    all_to_all x1, blocking collectives, on_device(): lax.all_to_all(send_x, 'expert', split_axis=0, concat_axis=0, tiled=True)  22.2 us
    all_to_all x1, blocking collectives, on_device(): lax.all_to_all(send_g, 'expert', split_axis=0, concat_axis=0, tiled=True)  15.8 us
    all_to_all x1, blocking collectives, on_device(): lax.all_to_all(send_p, 'expert', split_axis=0, concat_axis=0, tiled=True)  12.8 us
    all_to_all x1, starting transfers between devices, on_device(): lax.all_to_all(gate_dot.reshape(experts, capacity), 'expert', split_axis=...  9.85 us
    all_to_all x1, starting transfers between devices, on_device(): lax.all_to_all(row_grad.reshape(experts, capacity, width_part), 'expert',...  9.84 us
  transfers between devices with their start and end apart: 4, of which 4 were waited for; matrix products, arithmetic and copies ran while one was open for 2% of the time, Pallas kernels for 0%

profile of v1, /device:TPU:8, one launch (start us, length us, event | category | flops | bytes accessed | tf_op | source)
XLA Modules:
  0.0 350.9 jit_solution(5003342842120151398)
XLA Ops:
  7.2 0.0 copy-start
  7.2 0.0 copy-start.3
  7.2 0.0 all-reduce.3.cloned.1.call-start
  7.2 0.8 convert_reduce_fusion
  8.0 0.1 copy.46
  8.1 0.1 reduce_window_sum.11
  8.2 0.1 copy.48
  8.3 0.9 convolution_convert_fusion.6
  9.2 0.1 copy.51
  9.4 22.2 %all_to_all.37 = bf16[32,15,256]{2,1,0:T(8,128)(2,1)S(1)} all-to-all(bf16[32,15,256]{2,1,0:T(8,128)(2,1)S(1)} %copy.51), channel_id=1, replica_groups=mesh['dp'=16,'expert'=32] {'expert'}, dimensions={0} | all-to-all | bytes 491520 | tf_op jit(solution)/shard_map/all_to_all | solution.py:49
  31.6 0.1 reshape.59
  31.7 0.0 copy-done
  31.7 1.4 convolution_convert_fusion
  33.1 0.0 copy-done.3
  33.1 0.0 copy-start.5
  33.1 1.4 convolution_convert_fusion.1
  34.5 0.0 all-reduce.3.cloned.1.call-update
  34.5 0.0 copy-done.5
  34.5 0.2 convolution_convert_fusion.7
  34.7 0.1 copy.50
  34.9 15.8 %all_to_all.38 = bf16[32,15,256]{2,1,0:T(8,128)(2,1)S(1)} all-to-all(bf16[32,15,256]{2,1,0:T(8,128)(2,1)S(1)} %copy.50), channel_id=1, replica_groups=mesh['dp'=16,'expert'=32] {'expert'}, dimensions={0} | all-to-all | bytes 491520 | tf_op jit(solution)/shard_map/all_to_all | solution.py:50
  50.7 0.0 copy-start.2
  50.7 0.1 reshape.62
  50.8 0.0 copy-start.4
  50.8 104.4 %all-reduce.3.cloned.1.call-done = (bf16[480,1024]{1,0:T(8,128)(2,1)}, bf16[480,1024]{1,0:T(8,128)(2,1)}) async-done(((bf16[480,1024]{1,0:T(8,128)(2,1)}, bf16[480,1024]{1,0:T(8,128)(2,1)}), (bf16[480,1024]{1,0:T(8,128)(2,1)}, bf16[480,1024]{1,0:T(8,128)(2,1)})) %all-reduce.3.cloned.1.call-update) | async-done | bytes 1966096 | tf_op jit(solution)/shard_map/psum | solution.py:65
  155.2 2.1 fusion.3
  157.4 0.0 copy-start.1
  157.4 1.0 copy-done.1
  158.4 0.0 copy-done.2
  158.4 0.5 fusion.14
  158.9 0.0 copy-done.4
  158.9 26.2 %psum.23 = bf16[480]{0:T(512)(128)(2,1)S(1)} all-reduce(f32[480]{0:T(512)S(1)} %fusion.14), channel_id=1, replica_groups=mesh['dp'=16,'expert'=32] {'dp'}, use_global_device_ids=true, to_apply=%region_7.8 | all-reduce | flops 480 | bytes 2880 | tf_op jit(solution)/shard_map/psum | solution.py:71
  185.1 0.7 all_to_all.31
  185.9 9.8 %all-to-all-start.4 = ((bf16[32,1,15]{2,1,0:T(2,128)(2,1)}), bf16[32,1,15]{2,1,0:T(2,128)(2,1)S(1)}, u32[]{:S(2)}, u32[]{:S(2)}) async-start(bf16[32,1,15]{2,1,0:T(2,128)(2,1)} %all_to_all.31), calls=%async_computation.4 | async-start | bytes 32768 | tf_op jit(solution)/shard_map/all_to_all | solution.py:92
  195.7 0.0 all-gather.3.cloned.1.call-start
  195.8 0.0 copy-done.7
  195.8 8.4 %all-to-all-done.4 = bf16[32,1,15]{2,1,0:T(2,128)(2,1)S(1)} async-done(((bf16[32,1,15]{2,1,0:T(2,128)(2,1)}), bf16[32,1,15]{2,1,0:T(2,128)(2,1)S(1)}, u32[]{:S(2)}, u32[]{:S(2)}) %all-to-all-start.4) | async-done | bytes 992 | tf_op jit(solution)/shard_map/all_to_all | solution.py:92
  204.3 0.1 copy.54
  204.4 0.1 copy.58
  204.5 0.2 fusion.26
  204.7 0.0 copy-done.6
  204.7 0.6 fusion.33
  205.3 0.2 fusion.28
  205.5 0.1 copy.57
  205.6 0.1 copy.49
  205.7 12.8 %all_to_all.39 = bf16[32,1,15]{2,1,0:T(2,128)(2,1)S(1)} all-to-all(bf16[32,1,15]{2,1,0:T(2,128)(2,1)S(1)} %copy.49), channel_id=1, replica_groups=mesh['dp'=16,'expert'=32] {'expert'}, dimensions={0} | all-to-all | bytes 1920 | tf_op jit(solution)/shard_map/all_to_all | solution.py:51
  218.5 0.1 multiply_convert_fusion
  218.7 0.1 convert_element_type.116
  218.8 1.4 convolution_convert_fusion.2
  220.2 0.0 all-gather.3.cloned.1.call-update
  220.2 0.1 convert_reduce_fusion.1
  220.3 0.1 reshape.63
  220.4 86.1 %all-gather.3.cloned.1.call-done = bf16[7680,1024]{1,0:T(8,128)(2,1)} async-done(((bf16[480,1024]{1,0:T(8,128)(2,1)}), bf16[7680,1024]{1,0:T(8,128)(2,1)}) %all-gather.3.cloned.1.call-update) | async-done | bytes 15728656 | tf_op jit(solution)/shard_map/all_gather | solution.py:66
  306.4 9.7 %reduce_sum.50 = bf16[480,1024]{1,0:T(8,128)(2,1)} reduce(bf16[16,480,1024]{2,1,0:T(8,128)(2,1)} %bitcast.61, bf16[]{:T(256)} %constant.10.clone.1), dimensions={0}, to_apply=%region_3.4 | reduce | flops 7372800 | bytes 16711682 | tf_op jit(solution)/shard_map/reduce_sum | solution.py:66
  316.2 2.8 fusion.9
  319.0 0.5 fusion.16
  319.5 0.5 fusion.13
  319.9 0.8 reshape.60
  320.7 9.8 %all-to-all-start.3 = ((bf16[32,15,256]{2,1,0:T(8,128)(2,1)}), bf16[32,15,256]{2,1,0:T(8,128)(2,1)S(1)}, u32[]{:S(2)}, u32[]{:S(2)}) async-start(bf16[32,15,256]{2,1,0:T(8,128)(2,1)} %reshape.60), calls=%async_computation.3 | async-start | bytes 524288 | tf_op jit(solution)/shard_map/all_to_all | solution.py:85
  330.6 2.7 fusion.12
  333.3 1.3 fusion.10
  334.5 1.3 fusion.11
  335.8 7.5 %all-to-all-done.3 = bf16[32,15,256]{2,1,0:T(8,128)(2,1)S(1)} async-done(((bf16[32,15,256]{2,1,0:T(8,128)(2,1)}), bf16[32,15,256]{2,1,0:T(8,128)(2,1)S(1)}, u32[]{:S(2)}, u32[]{:S(2)}) %all-to-all-start.3) | async-done | bytes 245792 | tf_op jit(solution)/shard_map/all_to_all | solution.py:85
  343.3 0.8 fusion.15
  (8 shorter events, 0.1 us)
Async XLA Ops:
  7.2 24.5 %copy-start = (bf16[1,256,1024]{2,1,0:T(8,128)(2,1)S(1)}, bf16[1,256,1024]{2,1,0:T(8,128)(2,1)}, u32[]{:S(2)}) copy-start(bf16[1,256,1024]{2,1,0:T(8,128)(2,1)} %param.11) | copy-start | bytes 1572868
  7.2 25.9 %copy-start.3 = (bf16[1,256,1024]{2,1,0:T(8,128)(2,1)S(1)}, bf16[1,256,1024]{2,1,0:T(8,128)(2,1)}, u32[]{:S(2)}) copy-start(bf16[1,256,1024]{2,1,0:T(8,128)(2,1)} %param.12) | copy-start | bytes 1572868
  7.2 148.0 %all-reduce.3.cloned.1.call-start = ((), (), s32[]{:S(2)}) async-start(), calls=%async_computation.6 | async-start | bytes 3932160 | tf_op jit(solution)/shard_map/psum | solution.py:65
  33.1 1.4 copy-start.5
  50.7 107.6 %copy-start.2 = (bf16[1,1024,256]{2,1,0:T(8,128)(2,1)S(1)}, bf16[1,1024,256]{2,1,0:T(8,128)(2,1)}, u32[]{:S(2)}) copy-start(bf16[1,1024,256]{2,1,0:T(8,128)(2,1)} %param.13) | copy-start | bytes 1572868
  50.8 108.1 %copy-start.4 = (f32[480,256]{1,0:T(8,128)}, f32[480,256]{1,0:T(8,128)S(1)}, u32[]{:S(2)}) copy-start(f32[480,256]{1,0:T(8,128)S(1)} %reshape.62) | copy-start | bytes 1474564
  155.2 40.6 %copy-start.7 = (bf16[40,8]{0,1:T(8,128)(2,1)S(1)}, bf16[40,8]{0,1:T(8,128)(2,1)}, u32[]{:S(2)}) copy-start(bf16[40,8]{0,1:T(8,128)(2,1)} %param.10) | copy-start | bytes 1924
  155.2 49.4 %copy-start.6 = (s32[40,8]{0,1:T(8,128)S(1)}, s32[40,8]{0,1:T(8,128)}, u32[]{:S(2)}) copy-start(s32[40,8]{0,1:T(8,128)} %param.9) | copy-start | bytes 3844
  157.4 1.0 copy-start.1
  185.9 18.4 %all-to-all-start.4 = ((bf16[32,1,15]{2,1,0:T(2,128)(2,1)}), bf16[32,1,15]{2,1,0:T(2,128)(2,1)S(1)}, u32[]{:S(2)}, u32[]{:S(2)}) async-start(bf16[32,1,15]{2,1,0:T(2,128)(2,1)} %all_to_all.31), calls=%async_computation.4 | async-start | bytes 32768 | tf_op jit(solution)/shard_map/all_to_all | solution.py:92
  195.7 110.7 %all-gather.3.cloned.1.call-start = ((), (), s32[]{:S(2)}) async-start(), calls=%async_computation.5 | async-start | bytes 16711680 | tf_op jit(solution)/shard_map/all_gather | solution.py:66
  320.7 22.5 %all-to-all-start.3 = ((bf16[32,15,256]{2,1,0:T(8,128)(2,1)}), bf16[32,15,256]{2,1,0:T(8,128)(2,1)S(1)}, u32[]{:S(2)}, u32[]{:S(2)}) async-start(bf16[32,15,256]{2,1,0:T(8,128)(2,1)} %reshape.60), calls=%async_computation.3 | async-start | bytes 524288 | tf_op jit(solution)/shard_map/all_to_all | solution.py:85
Sparse Core Ops, SparseCore 0:
  34.6 120.5 all-reduce.2
  220.3 86.0 all-gather.2
